TPU v7x, 128 devices: a whole 4x4x4 slice. The times are simulated.
128 devices in a mesh: dp: 32 (over y, z, core), tensor: 4 (over x).
Axes of the slice: x: 4, y: 4, z: 4, core: 2. Of those that a mesh axis runs over, the one named last changes fastest.
Arguments:
- tokens: bfloat16 [16384, 4096], P('dp', 'tensor'), may hold values from -6 to 6
- grad_out: bfloat16 [16384, 4096], P('dp'), may hold values from -3 to 3
- gate_pre: bfloat16 [16384, 14336], P('dp', 'tensor'), may hold values from -9 to 9
- up_value: bfloat16 [16384, 14336], P('dp', 'tensor'), may hold values from -6 to 6
- down_weight: bfloat16 [14336, 4096], P('tensor', 'dp'), may hold values from -0.09375 to 0.09375
- in_proj: bfloat16 [128, 4096], P(None, 'tensor'), may hold values from -0.09375 to 0.09375
- out_proj: bfloat16 [128, 14336], P(None, 'tensor'), may hold values from -0.046875 to 0.046875
- test_matrix: bfloat16 [16384, 128], replicated, may hold values from -0.046875 to 0.046875
Outputs:
- factor: float32 [16384, 128], P(('dp', 'tensor'))
All inputs are finite; a program needn't handle non-finite values.
Results may differ from a plain program's by a relative error of at most 0.0065.
The roundings to bfloat16 on the way count: a program that leaves them out, or rounds other values in their place, can miss the bound.
Values may be sent and summed in bfloat16 or wider, within the bound.
A program may use at most 128 MiB of HBM per device.

v0:
```python
import jax
import jax.numpy as jnp
from jax import lax
from jax.sharding import PartitionSpec as P

SEQ_LEN = 128
shift_scale = 0.1
tiny_value = 1e-06


def local(tokens, grad_out, gate_pre, up_value, down_weight, in_proj, out_proj, test_matrix):
    rows = grad_out.shape[0]
    hidden_grad = lax.dot_general(
        grad_out,
        lax.all_gather(down_weight, "dp", axis=1, tiled=True),
        (((1,), (1,)), ((), ())),
        preferred_element_type=jnp.float32,
    )
    gate_wide = gate_pre.astype(jnp.float32)
    logistic = jax.nn.sigmoid(gate_wide)
    gate_grad = (
        hidden_grad * up_value.astype(jnp.float32) * logistic * (1.0 + gate_wide * (1.0 - logistic))
    ).astype(jnp.bfloat16)
    act_part = lax.dot_general(
        tokens, in_proj, (((1,), (1,)), ((), ())), preferred_element_type=jnp.float32
    )
    out_part = lax.dot_general(
        gate_grad, out_proj, (((1,), (1,)), ((), ())), preferred_element_type=jnp.float32
    )
    act_sum, out_sum = lax.psum((act_part, out_part), "tensor")
    pdim = in_proj.shape[0]
    rank_cols = test_matrix.shape[1]
    seqs_here = rows // SEQ_LEN
    act_seq = act_sum.astype(jnp.bfloat16).reshape(seqs_here, SEQ_LEN, pdim)
    out_seq = out_sum.astype(jnp.bfloat16).reshape(seqs_here, SEQ_LEN, pdim)
    proj_grad = (
        jnp.einsum("slp,slq->spq", act_seq, out_seq, preferred_element_type=jnp.float32)
        .astype(jnp.bfloat16)
        .reshape(seqs_here, pdim * pdim)
    )
    coeff = jnp.dot(proj_grad, test_matrix, preferred_element_type=jnp.float32).astype(jnp.bfloat16)
    dp_count = lax.axis_size("dp")
    tp_count = lax.axis_size("tensor")
    tp_index = lax.axis_index("tensor")
    dp_index = lax.axis_index("dp")
    width = pdim * pdim // (dp_count * tp_count)
    picked = lax.dynamic_slice_in_dim(
        proj_grad.reshape(seqs_here, dp_count, tp_count, width), tp_index, 1, 2
    ).reshape(seqs_here, dp_count * width)
    omega_wide = test_matrix.astype(jnp.float32)
    omega_picked = lax.dynamic_slice_in_dim(
        omega_wide.reshape(dp_count, tp_count, width, rank_cols), tp_index, 1, 1
    ).reshape(dp_count * width, rank_cols)
    omega_own = lax.dynamic_slice_in_dim(omega_picked, dp_index * width, width, 0)
    sketch_part = lax.dot_general(
        picked, coeff, (((0,), (0,)), ((), ())), preferred_element_type=jnp.float32
    )
    gram = lax.dot_general(
        test_matrix, test_matrix, (((0,), (0,)), ((), ())), preferred_element_type=jnp.float32
    )
    omega_sq = jnp.trace(gram)
    summed = lax.psum(sketch_part, "dp")
    core_local = lax.dot_general(
        omega_picked, summed, (((0,), (0,)), ((), ())), precision=lax.Precision.HIGHEST
    )
    square_sum, core_sketch = lax.psum((jnp.sum(summed * summed), core_local), "tensor")
    own_rows = lax.dynamic_slice_in_dim(summed, dp_index * width, width, 0)
    shift = shift_scale * jnp.sqrt(square_sum / (omega_sq + tiny_value))
    core = core_sketch + shift * gram
    core = 0.5 * (core + core.T)
    lower = jnp.linalg.cholesky(core)
    shifted = own_rows + shift * omega_own
    factor = jax.scipy.linalg.solve_triangular(lower, shifted.T, lower=True).T
    return factor


def solution(mesh):
    in_specs = (
        P("dp", "tensor"),
        P("dp", None),
        P("dp", "tensor"),
        P("dp", "tensor"),
        P("tensor", "dp"),
        P(None, "tensor"),
        P(None, "tensor"),
        P(),
    )
    out_specs = P(("dp", "tensor"), None)
    return jax.shard_map(local, mesh=mesh, in_specs=in_specs, out_specs=out_specs, check_vma=False)
```

profile of v0, /device:TPU:0, one launch (start us, length us, event | category | flops | bytes accessed | tf_op | source)
XLA Modules:
  0.0 362.2 jit_solution(9847140538251873871)
XLA Ops:
  6.5 0.7 all-gather.2.cloned.1.call-update
  7.3 0.5 copy-done
  7.8 1.4 fusion.24
  9.1 116.3 %all-gather.2.cloned.1.call-done = bf16[3584,4096]{1,0:T(8,128)(2,1)} async-done(((bf16[3584,128]{1,0:T(8,128)(2,1)}), bf16[3584,4096]{1,0:T(8,128)(2,1)}) %all-gather.2.cloned.1.call-update) | async-done | bytes 29360144 | tf_op jit(solution)/shard_map/all_gather | solution.py:15
  125.4 24.7 %fusion.25 = f32[512,128]{1,0:T(8,128)S(1)} fusion(bf16[128,3584]{1,0:T(8,128)(2,1)} %param.14, bf16[512,3584]{1,0:T(8,128)(2,1)} %param.10, bf16[512,3584]{1,0:T(8,128)(2,1)} %param.11, bf16[512,4096]{1,0:T(8,128)(2,1)} %param.9, bf16[3584,4096]{1,0:T(8,128)(2,1)} %all-gather.2.cloned.1.call-done), kind=kOutput, calls=%fused_computation.40 | convolution fusion | flops 15524167680 | bytes 42074112 | tf_op jit(solution)/shard_map/dot_general | solution.py:27
  150.1 23.1 %all-reduce.8 = (bf16[512,128]{1,0:T(8,128)(2,1)S(1)}, bf16[512,128]{1,0:T(8,128)(2,1)S(1)}) all-reduce(f32[512,128]{1,0:T(8,128)S(1)} %fusion.24, f32[512,128]{1,0:T(8,128)S(1)} %fusion.25), channel_id=1, replica_groups=mesh['dp'=32,'tensor'=4] {'tensor'}, use_global_device_ids=true, to_apply=%region_0.0 | all-reduce | flops 131072 | bytes 786432 | tf_op jit(solution)/shard_map/psum | solution.py:30
  173.2 0.2 convolution_convert_fusion
  173.6 4.7 %fusion.6 = f32[4096,128]{0,1:T(8,128)} fusion(bf16[16384,128]{1,0:T(8,128)(2,1)} %param.15, bf16[1,4,128,128]{3,2,1,0:T(8,128)(2,1)S(1)} %bitcast.60, bf16[1,4,32,128]{3,2,1,0:T(8,128)(2,1)S(1)} %bitcast.61), kind=kOutput, calls=%fused_computation.12 | convolution fusion | flops 20972032 | bytes 6455296 | tf_op jit(solution)/shard_map/dot_general | solution.py:55
  178.6 5.4 %select_reduce_fusion.1 = (f32[]{:T(128)}, f32[128,128]{1,0:T(8,128)S(1)}) fusion(bf16[16384,128]{1,0:T(8,128)(2,1)} %param.15), kind=kOutput, calls=%fused_computation.29 | convolution fusion | flops 536920064 | bytes 4259844 | tf_op jit(solution)/shard_map/dot_general | solution.py:58
  184.0 1.3 constant_dynamic-slice_fusion
  185.3 1.0 copy.28
  186.3 0.3 reshape.38
  186.6 2.9 copy.42
  189.5 96.2 %all-reduce.5.cloned.1.call-done = f32[4096,128]{0,1:T(8,128)} async-done(((f32[4096,128]{0,1:T(8,128)}), f32[4096,128]{0,1:T(8,128)}) %all-reduce.5.cloned.1.call-update) | async-done | bytes 2097168 | tf_op jit(solution)/shard_map/psum | solution.py:62
  285.7 3.3 fusion.26
  289.1 2.7 multiply_reduce_fusion
  292.4 10.9 %psum.38 = f32[]{:T(128)} all-reduce(f32[]{:T(128)} %multiply_reduce_fusion), channel_id=1, replica_groups=mesh['dp'=32,'tensor'=4] {'tensor'}, use_global_device_ids=true, to_apply=%region_4.5 | all-reduce | flops 1 | bytes 8 | tf_op jit(solution)/shard_map/psum | solution.py:66
  303.9 26.1 %all-reduce.7.cloned.1.call-done = f32[128,128]{0,1:T(8,128)} async-done(((f32[128,128]{0,1:T(8,128)}), f32[128,128]{0,1:T(8,128)}) %all-reduce.7.cloned.1.call-update) | async-done | bytes 65552 | tf_op jit(solution)/shard_map/psum | solution.py:66
  330.0 0.8 multiply_add_fusion
  331.0 11.7 %cholesky.13 = f32[128,128]{1,0:T(8,128)S(1)} custom-call(f32[128,128]{1,0:T(8,128)S(1)} %fusion.14), custom_call_target="Cholesky" | custom-call | tf_op jit(solution)/shard_map/jit(cholesky)/cholesky | solution.py:71
  342.8 0.6 compare_reduce_fusion
  343.4 0.7 fusion.11
  344.1 9.8 %custom-call.7 = f32[1,128,128]{1,2,0:T(8,128)S(1)} custom-call(f32[1,128,128]{2,1,0:T(8,128)S(1)} %fusion.11), custom_call_target="InvertDiagBlocksLowerTriangular" | custom-call | tf_op jit(solution)/shard_map/jit(_solve_triangular)/triangular_solve | solution.py:73
  353.9 1.8 fusion.12
  (13 shorter events, 0.8 us)
Async XLA Ops:
  6.5 1.2 copy-start
  6.5 118.9 %all-gather.2.cloned.1.call-start = ((), (), s32[]{:S(2)}) async-start(), calls=%async_computation | async-start | bytes 30277632 | tf_op jit(solution)/shard_map/all_gather | solution.py:15
  7.3 278.4 %all-reduce.5.cloned.1.call-start = ((), (), s32[]{:S(2)}) async-start(), calls=%async_computation.1 | async-start | bytes 4194304 | tf_op jit(solution)/shard_map/psum | solution.py:62
  178.3 151.6 %all-reduce.7.cloned.1.call-start = ((), (), s32[]{:S(2)}) async-start(), calls=%async_computation.2 | async-start | bytes 131072 | tf_op jit(solution)/shard_map/psum | solution.py:66
Sparse Core Ops, SparseCore 0:
  9.5 115.8 all-gather.1
  178.4 107.2 all-reduce.4
  289.2 40.7 all-reduce.6
where the time goes:
time: 363 us; the launch traced here: 362 us
  waiting for transfers between devices  239 us (66%)
  matrix products  41.5 us (11%)
  blocking collectives  34 us (9%)
  other arithmetic  26.7 us (7%)
  between operations  14.4 us (4%)
  local copies, waits for them, and re-layouts  6.14 us (2%)
    all_gather x1, waiting for transfers between devices, local(): lax.all_gather(down_weight, 'dp', axis=1, tiled=True)  116 us
    psum x1, waiting for transfers between devices, local(): summed = lax.psum(sketch_part, 'dp')  96.2 us
    psum x1, waiting for transfers between devices, local(): lax.psum((jnp.sum(summed * summed), core_local), 'tensor')  26.1 us
    dot_general x1, matrix products, local(): lax.dot_general(gate_grad, out_proj, (((1,), (1,)), ((), ())), preferred_...  24.7 us
    psum x1, blocking collectives, local(): act_sum, out_sum = lax.psum((act_part, out_part), 'tensor')  23.1 us
    another operation x3, other arithmetic, local(): lower = jnp.linalg.cholesky(core)  12.4 us
    psum x1, blocking collectives, local(): lax.psum((jnp.sum(summed * summed), core_local), 'tensor')  10.9 us
    another operation x2, other arithmetic, local(): factor = jax.scipy.linalg.solve_triangular(lower, shifted.T, lower=True).T  10.5 us
  transfers between devices with their start and end apart: 3, of which 3 were waited for; matrix products, arithmetic and copies ran while one was open for 4% of the time, Pallas kernels for 0%

commit v1 on v0

--- a/solution.py
+++ b/solution.py
@@ -59,7 +59,9 @@
         test_matrix, test_matrix, (((0,), (0,)), ((), ())), preferred_element_type=jnp.float32
     )
     omega_sq = jnp.trace(gram)
-    summed = lax.psum(sketch_part, "dp")
+    summed = sketch_part
+    for hop in (1, 2, 4, 8, 16):
+        summed = summed + lax.ppermute(summed, "dp", [(dev, dev ^ hop) for dev in range(32)])
     core_local = lax.dot_general(
         omega_picked, summed, (((0,), (0,)), ((), ())), precision=lax.Precision.HIGHEST
     )

time: 363 us -> 448 us (1.23)
  waiting for transfers between devices: 239 us -> 319 us
  starting transfers between devices: 0.26 us -> 9.55 us
    ppermute x0 -> x5, waiting for transfers between devices: none -> 182 us  [local(): lax.ppermute(summed, 'dp', [(dev, dev ^ hop) for dev in range(32)])]
    psum x1 -> x0, waiting for transfers between devices: 96.2 us -> none  [local(): summed = lax.psum(sketch_part, 'dp')]
    ppermute x0 -> x5, starting transfers between devices: none -> 9.51 us  [local(): lax.ppermute(summed, 'dp', [(dev, dev ^ hop) for dev in range(32)])]
    psum x1, waiting for transfers between devices: 26.1 us -> 19.4 us  [local(): lax.psum((jnp.sum(summed * summed), core_local), 'tensor')]
  transfers between devices with their start and end apart: 3 -> 7, of which waited for: 3 -> 7; matrix products, arithmetic and copies ran while one was open for 4% -> 3% of each run, Pallas kernels for 0% -> 0%
where the time goes in v1:
time: 448 us
  waiting for transfers between devices  319 us (71%)
  matrix products  38.5 us (9%)
  blocking collectives  31.3 us (7%)
  other arithmetic  27.6 us (6%)
  between operations  14.9 us (3%)
  starting transfers between devices  9.55 us (2%)
  local copies, waits for them, and re-layouts  6.97 us (2%)
    ppermute x5, waiting for transfers between devices, local(): lax.ppermute(summed, 'dp', [(dev, dev ^ hop) for dev in range(32)])  182 us
    all_gather x1, waiting for transfers between devices, local(): lax.all_gather(down_weight, 'dp', axis=1, tiled=True)  116 us
    dot_general x1, matrix products, local(): lax.dot_general(gate_grad, out_proj, (((1,), (1,)), ((), ())), preferred_...  24.7 us
    psum x1, blocking collectives, local(): act_sum, out_sum = lax.psum((act_part, out_part), 'tensor')  23.1 us
    psum x1, waiting for transfers between devices, local(): lax.psum((jnp.sum(summed * summed), core_local), 'tensor')  19.4 us
    another operation x3, other arithmetic, local(): lower = jnp.linalg.cholesky(core)  12.4 us
    another operation x2, other arithmetic, local(): factor = jax.scipy.linalg.solve_triangular(lower, shifted.T, lower=True).T  10.5 us
    ppermute x5, starting transfers between devices, local(): lax.ppermute(summed, 'dp', [(dev, dev ^ hop) for dev in range(32)])  9.51 us
  transfers between devices with their start and end apart: 7, of which 7 were waited for; matrix products, arithmetic and copies ran while one was open for 3% of the time, Pallas kernels for 0%

profile of v1, /device:TPU:0, one launch (start us, length us, event | category | flops | bytes accessed | tf_op | source)
XLA Modules:
  0.0 447.6 jit_solution(15350555425189564253)
XLA Ops:
  7.8 1.4 fusion.24
  9.1 116.3 %all-gather.2.cloned.1.call-done = bf16[3584,4096]{1,0:T(8,128)(2,1)} async-done(((bf16[3584,128]{1,0:T(8,128)(2,1)}), bf16[3584,4096]{1,0:T(8,128)(2,1)}) %all-gather.2.cloned.1.call-update) | async-done | bytes 29360144 | tf_op jit(solution)/shard_map/all_gather | solution.py:15
  125.4 24.7 %fusion.25 = f32[512,128]{1,0:T(8,128)S(1)} fusion(bf16[128,3584]{1,0:T(8,128)(2,1)} %param.14, bf16[512,3584]{1,0:T(8,128)(2,1)} %param.10, bf16[512,3584]{1,0:T(8,128)(2,1)} %param.11, bf16[512,4096]{1,0:T(8,128)(2,1)} %param.9, bf16[3584,4096]{1,0:T(8,128)(2,1)} %all-gather.2.cloned.1.call-done), kind=kOutput, calls=%fused_computation.40 | convolution fusion | flops 15524167680 | bytes 42074112 | tf_op jit(solution)/shard_map/dot_general | solution.py:27
  150.1 23.1 %all-reduce.5 = (bf16[512,128]{1,0:T(8,128)(2,1)S(1)}, bf16[512,128]{1,0:T(8,128)(2,1)S(1)}) all-reduce(f32[512,128]{1,0:T(8,128)S(1)} %fusion.24, f32[512,128]{1,0:T(8,128)S(1)} %fusion.25), channel_id=1, replica_groups=mesh['dp'=32,'tensor'=4] {'tensor'}, use_global_device_ids=true, to_apply=%region_0.0 | all-reduce | flops 131072 | bytes 786432 | tf_op jit(solution)/shard_map/psum | solution.py:30
  173.7 3.3 fusion.6
  177.1 4.1 collective-permute-done
  181.5 1.6 collective-permute-start.1
  183.1 46.1 %collective-permute-done.1 = f32[4096,128]{0,1:T(8,128)S(1)} collective-permute-done((f32[4096,128]{0,1:T(8,128)S(1)}, f32[4096,128]{0,1:T(8,128)S(1)}, u32[]{:S(2)}, u32[]{:S(2)}) %collective-permute-start.1) | collective-permute-done | bytes 2097184 | tf_op jit(solution)/shard_map/ppermute | solution.py:64
  229.5 2.9 collective-permute-start.2
  232.4 45.5 %collective-permute-done.2 = f32[4096,128]{0,1:T(8,128)S(1)} collective-permute-done((f32[4096,128]{0,1:T(8,128)S(1)}, f32[4096,128]{0,1:T(8,128)S(1)}, u32[]{:S(2)}, u32[]{:S(2)}) %collective-permute-start.2) | collective-permute-done | bytes 2097184 | tf_op jit(solution)/shard_map/ppermute | solution.py:64
  278.2 1.6 collective-permute-start.3
  279.8 44.5 %collective-permute-done.3 = f32[4096,128]{0,1:T(8,128)S(1)} collective-permute-done((f32[4096,128]{0,1:T(8,128)S(1)}, f32[4096,128]{0,1:T(8,128)S(1)}, u32[]{:S(2)}, u32[]{:S(2)}) %collective-permute-start.3) | collective-permute-done | bytes 2097184 | tf_op jit(solution)/shard_map/ppermute | solution.py:64
  324.5 3.3 collective-permute-start.4
  329.1 42.2 %collective-permute-done.4 = f32[4096,128]{0,1:T(8,128)S(1)} collective-permute-done((f32[4096,128]{0,1:T(8,128)S(1)}, f32[4096,128]{0,1:T(8,128)S(1)}, u32[]{:S(2)}, u32[]{:S(2)}) %collective-permute-start.4) | collective-permute-done | bytes 2097184 | tf_op jit(solution)/shard_map/ppermute | solution.py:64
  372.6 1.8 fusion.26
  374.3 5.4 %select_reduce_fusion.1 = (f32[]{:T(128)}, f32[128,128]{1,0:T(8,128)S(1)}) fusion(bf16[16384,128]{1,0:T(8,128)(2,1)} %param.15), kind=kOutput, calls=%fused_computation.29 | convolution fusion | flops 536920064 | bytes 4259844 | tf_op jit(solution)/shard_map/dot_general | solution.py:58
  379.7 1.7 copy.30
  381.6 1.6 reshape.38
  383.1 3.0 copy.44
  386.8 8.3 %psum.30 = f32[]{:T(128)} all-reduce(f32[]{:T(128)} %get-tuple-element.7), channel_id=1, replica_groups=mesh['dp'=32,'tensor'=4] {'tensor'}, use_global_device_ids=true, to_apply=%region_3.4 | all-reduce | flops 1 | bytes 8 | tf_op jit(solution)/shard_map/psum | solution.py:68
  395.7 19.4 %all-reduce.4.cloned.1.call-done = f32[128,128]{0,1:T(8,128)} async-done(((f32[128,128]{0,1:T(8,128)}), f32[128,128]{0,1:T(8,128)}) %all-reduce.4.cloned.1.call-update) | async-done | bytes 65552 | tf_op jit(solution)/shard_map/psum | solution.py:68
  416.2 11.7 %cholesky.13 = f32[128,128]{1,0:T(8,128)S(1)} custom-call(f32[128,128]{1,0:T(8,128)S(1)} %fusion.14), custom_call_target="Cholesky" | custom-call | tf_op jit(solution)/shard_map/jit(cholesky)/cholesky | solution.py:73
  429.2 9.8 %custom-call.7 = f32[1,128,128]{1,2,0:T(8,128)S(1)} custom-call(f32[1,128,128]{2,1,0:T(8,128)S(1)} %fusion.11), custom_call_target="InvertDiagBlocksLowerTriangular" | custom-call | tf_op jit(solution)/shard_map/jit(_solve_triangular)/triangular_solve | solution.py:75
  439.0 1.8 fusion.12
  (26 shorter events, 7.8 us)
Async XLA Ops:
  6.5 1.2 copy-start
  6.5 118.9 %all-gather.2.cloned.1.call-start = ((), (), s32[]{:S(2)}) async-start(), calls=%async_computation | async-start | bytes 30277632 | tf_op jit(solution)/shard_map/all_gather | solution.py:15
  7.3 407.8 %all-reduce.4.cloned.1.call-start = ((), (), s32[]{:S(2)}) async-start(), calls=%async_computation.1 | async-start | bytes 131072 | tf_op jit(solution)/shard_map/psum | solution.py:68
  177.0 4.2 collective-permute-start
  181.5 47.8 %collective-permute-start.1 = (f32[4096,128]{0,1:T(8,128)S(1)}, f32[4096,128]{0,1:T(8,128)S(1)}, u32[]{:S(2)}, u32[]{:S(2)}) collective-permute-start(f32[4096,128]{0,1:T(8,128)S(1)} %add.64), channel_id=1, source_target_pairs={{0,8},{4,12},{8,0},{12,4},{16,24},{20,28},{24,16},{28,20},{32,40},... | collective-permute-start | bytes 6291464 | tf_op jit(solution)/shard_map/ppermute | solution.py:64
  229.5 48.4 %collective-permute-start.2 = (f32[4096,128]{0,1:T(8,128)S(1)}, f32[4096,128]{0,1:T(8,128)S(1)}, u32[]{:S(2)}, u32[]{:S(2)}) collective-permute-start(f32[4096,128]{0,1:T(8,128)S(1)} %add.65), channel_id=1, source_target_pairs={{0,16},{4,20},{8,24},{12,28},{16,0},{20,4},{24,8},{28,12},{32,48},... | collective-permute-start | bytes 6291464 | tf_op jit(solution)/shard_map/ppermute | solution.py:64
  278.2 46.0 %collective-permute-start.3 = (f32[4096,128]{0,1:T(8,128)S(1)}, f32[4096,128]{0,1:T(8,128)S(1)}, u32[]{:S(2)}, u32[]{:S(2)}) collective-permute-start(f32[4096,128]{0,1:T(8,128)S(1)} %add.66), channel_id=1, source_target_pairs={{0,32},{4,36},{8,40},{12,44},{16,48},{20,52},{24,56},{28,60},{32,0... | collective-permute-start | bytes 6291464 | tf_op jit(solution)/shard_map/ppermute | solution.py:64
  324.5 46.9 %collective-permute-start.4 = (f32[4096,128]{0,1:T(8,128)S(1)}, f32[4096,128]{0,1:T(8,128)S(1)}, u32[]{:S(2)}, u32[]{:S(2)}) collective-permute-start(f32[4096,128]{0,1:T(8,128)S(1)} %add.67), channel_id=1, source_target_pairs={{0,64},{4,68},{8,72},{12,76},{16,80},{20,84},{24,88},{28,92},{32,9... | collective-permute-start | bytes 6291464 | tf_op jit(solution)/shard_map/ppermute | solution.py:64
  381.5 59.3 %copy-start.1 = (bf16[512,1024]{1,0:T(8,128)(2,1)S(1)}, bf16[512,1024]{1,0:T(8,128)(2,1)}, u32[]{:S(2)}) copy-start(bf16[512,1024]{1,0:T(8,128)(2,1)} %param.8) | copy-start | bytes 3145732
Sparse Core Ops, SparseCore 0:
  9.5 115.8 all-gather.1
  374.5 40.5 all-reduce.3
